TPU v7x, 32 devices: a whole 2x2x4 slice. The times are simulated.
32 devices in a mesh: group: 2 (over y), ctx: 4 (over z), head: 2 (over x), req: 2 (over core).
Axes of the slice: x: 2, y: 2, z: 4, core: 2. Of those that a mesh axis runs over, the one named last changes fastest.
Arguments:
- kda_query: bfloat16 [4, 768, 4096], P(('group', 'req'), 'ctx', 'head'), parts along dimension 0, may hold values from -6 to 6
- kda_key: bfloat16 [4, 768, 4096], P(('group', 'req'), 'ctx', 'head'), parts along dimension 0, may hold values from -6 to 6
- kda_value: bfloat16 [4, 768, 4096], P(('group', 'req'), 'ctx', 'head'), parts along dimension 0, may hold values from -6 to 6
- log_decay: bfloat16 [4, 768, 4096], P(('group', 'req'), 'ctx', 'head'), parts along dimension 0, may hold values from -1 to 0
- write_strength: float32 [4, 32, 768], P(('group', 'req'), 'head', 'ctx'), parts along dimension 0, may hold values from 0.1 to 0.95
- mla_query: bfloat16 [4, 768, 18432], P(('group', 'req'), 'ctx', 'head'), parts along dimension 0, may hold values from -18 to 18
- latents: bfloat16 [4, 768, 576], P(('group', 'req'), 'ctx'), parts along dimension 0, may hold values from -8 to 8
- value_up: bfloat16 [32, 512, 128], P('head'), may hold values from -0.25 to 0.25
- out_proj: bfloat16 [4096, 2304], P('head'), may hold values from -0.09375 to 0.09375
- doc_lengths: int32 [4, 8], P(('group', 'req')), parts along dimension 0, may hold values from 1 to 288, 768 in all within a row
Outputs:
- kda_out: bfloat16 [4, 768, 4096], P(('group', 'req'), 'ctx', 'head'), parts along dimension 0
- mixed: bfloat16 [4, 768, 2304], P(('group', 'req'), ('ctx', 'head')), parts along dimension 0
There are 2 independent parts, one for each index of `group`. A program takes and returns all parts, laid end to end along the dimension named above; an argument that names none is the same for every part. Nothing has to cross between parts.
Inputs may be any that keep to these rules, and one draw needn't show every extreme that they name: `doc_lengths`: each row's lengths sum to 768, and each row's longest prompt has exactly 288 positions.
All inputs are finite; a program needn't handle non-finite values.
Results may differ from a plain program's by a relative error of at most 0.009.
Values may be sent and summed in bfloat16 or wider, within the bound.
A program may use at most 128 MiB of HBM per device.

v0:
```python
import math
import jax
import jax.numpy as jnp
from jax import lax
from jax.sharding import PartitionSpec as P

ROPE = 64
NOPE = 128
SPAN = 64
top_value = lax.Precision.HIGHEST
masked_score = -1e30


def from_behind(value, axis, by):
    peers = lax.axis_size(axis)
    pairs = [(i, i + by) for i in range(peers) if 0 <= i + by < peers]
    return lax.ppermute(value, axis, pairs)


def unit_length(values):
    return values * lax.rsqrt(jnp.sum(values * values, axis=-1, keepdims=True) + 1e-06)


def doc_index(position_list, doc_ends):
    return jnp.sum((doc_ends[None, :] <= position_list[:, None]).astype(jnp.int32), axis=1)


def span_terms(query_rows, key_rows, value_rows, decay_rows, strength, doc_ids, prev_doc):
    span_len = key_rows.shape[1]
    state_dim = key_rows.shape[2]
    row_index = jnp.arange(span_len, dtype=jnp.int32)
    inclusive = (row_index[:, None] >= row_index[None, :]).astype(jnp.float32)
    summed = jnp.einsum("ij,hjc->hic", inclusive, decay_rows, precision=top_value)
    growth = jnp.exp(summed)
    key_hat = key_rows * growth
    key_tilde = key_rows * jnp.exp(-summed)
    query_estimate = query_rows * growth
    same_doc = doc_ids[:, None] == doc_ids[None, :]
    strict = same_doc & (row_index[:, None] > row_index[None, :])
    up_to = same_doc & (row_index[:, None] >= row_index[None, :])
    carried = (doc_ids == prev_doc).astype(jnp.float32)
    inner = jnp.einsum("hic,hjc->hij", key_hat, key_tilde, precision=top_value)
    lower_part = jnp.where(strict[None], inner * strength[:, :, None], 0.0)
    system = lower_part + jnp.eye(span_len, dtype=jnp.float32)[None]
    right_side = jnp.concatenate(
        [(strength * carried[None])[:, :, None] * key_hat, strength[:, :, None] * value_rows],
        axis=2,
    )
    solved = lax.linalg.triangular_solve(
        system, right_side, left_side=True, lower=True, unit_diagonal=True
    )
    weighted_key_rows = solved[:, :, :state_dim]
    update_rows = solved[:, :, state_dim:]
    attend = jnp.where(
        up_to[None], jnp.einsum("hic,hjc->hij", query_estimate, key_tilde, precision=top_value), 0.0
    )
    tail_mask = same_doc[span_len - 1].astype(jnp.float32)
    key_decay = key_rows * jnp.exp(summed[:, span_len - 1 :, :] - summed) * tail_mask[None, :, None]
    diagonal = (
        carried[span_len - 1]
        * growth[:, span_len - 1, :, None]
        * jnp.eye(state_dim, dtype=jnp.float32)[None]
    )
    transition = diagonal - jnp.einsum(
        "hjc,hjd->hcd", key_decay, weighted_key_rows, precision=top_value
    )
    offset = jnp.einsum("hjc,hjv->hcv", key_decay, update_rows, precision=top_value)
    return (query_estimate, carried, weighted_key_rows, update_rows, attend, transition, offset)


def span_output(terms, inbound_state):
    query_estimate, carried, weighted_key_rows, update_rows, attend, transition, offset = terms
    adjusted_rows = update_rows - jnp.einsum(
        "izy,iyn->izn", weighted_key_rows, inbound_state, precision=top_value
    )
    state_contribution = jnp.einsum(
        "izy,iyn->izn", query_estimate, inbound_state, precision=top_value
    )
    return carried[None, :, None] * state_contribution + jnp.einsum(
        "hij,hjv->hiv", attend, adjusted_rows, precision=top_value
    )


def apply_map(transition, offset, inbound_state):
    return jnp.einsum("hcd,hdv->hcv", transition, inbound_state, precision=top_value) + offset


def local(
    kda_query,
    kda_key,
    kda_value,
    log_decay,
    write_strength,
    mla_query,
    latents,
    value_up,
    out_proj,
    doc_lengths,
):
    tokens_dev = kda_query.shape[1]
    heads_dev = write_strength.shape[1]
    state_dim = kda_query.shape[2] // heads_dev
    ctx_count = lax.axis_size("ctx")
    ctx_place = lax.axis_index("ctx")
    first_pos = ctx_place * tokens_dev
    positions = first_pos + jnp.arange(tokens_dev, dtype=jnp.int32)
    doc_ends = jnp.cumsum(doc_lengths[0])
    doc_ids = doc_index(positions, doc_ends)

    def head_first(packed):
        return jnp.transpose(
            packed[0].astype(jnp.float32).reshape(tokens_dev, heads_dev, state_dim), (1, 0, 2)
        )

    query_rows = unit_length(head_first(kda_query))
    key_rows = unit_length(head_first(kda_key))
    value_rows = head_first(kda_value)
    decay_rows = head_first(log_decay)
    strength = write_strength[0]
    span_list = []
    eye_batch = jnp.broadcast_to(
        jnp.eye(state_dim, dtype=jnp.float32), (heads_dev, state_dim, state_dim)
    )
    transition = eye_batch
    offset = jnp.zeros((heads_dev, state_dim, state_dim), jnp.float32)
    for span_begin in range(0, tokens_dev, SPAN):
        span_stop = span_begin + SPAN
        prev_doc = doc_index(positions[span_begin : span_begin + 1] - 1, doc_ends)[0]
        terms = span_terms(
            query_rows[:, span_begin:span_stop],
            key_rows[:, span_begin:span_stop],
            value_rows[:, span_begin:span_stop],
            decay_rows[:, span_begin:span_stop],
            strength[:, span_begin:span_stop],
            doc_ids[span_begin:span_stop],
            prev_doc,
        )
        span_list.append(terms)
        offset = apply_map(terms[5], terms[6], offset)
        transition = jnp.einsum("hcd,hde->hce", terms[5], transition, precision=top_value)

    def relay(turn_index, inbound_state):
        outgoing = apply_map(transition, offset, inbound_state)
        return from_behind(outgoing.astype(jnp.bfloat16), "ctx", 1).astype(outgoing.dtype)

    inbound_state = lax.fori_loop(0, ctx_count - 1, relay, jnp.zeros_like(offset))
    pieces = []
    state_now = inbound_state
    for span_number, terms in enumerate(span_list):
        pieces.append(span_output(terms, state_now))
        if span_number + 1 < len(span_list):
            state_now = apply_map(terms[5], terms[6], state_now)
    kda_out = (
        jnp.transpose(jnp.concatenate(pieces, axis=1), (1, 0, 2))
        .reshape(1, tokens_dev, heads_dev * state_dim)
        .astype(jnp.bfloat16)
    )
    width = latents.shape[2]
    lat_dim = value_up.shape[1]
    score_scale = 1.0 / math.sqrt(NOPE + ROPE)
    query_flat = mla_query[0].reshape(tokens_dev * heads_dev, width)
    row_pos = jnp.repeat(positions, heads_dev)
    row_doc = jnp.repeat(doc_ids, heads_dev)
    row_total_count = tokens_dev * heads_dev
    row_peak = jnp.full((row_total_count,), masked_score, jnp.float32)
    block_rows = lax.all_gather(latents, "ctx", axis=1, tiled=True)[0]
    row_count = block_rows.shape[0]
    key_pos = jnp.arange(row_count, dtype=jnp.int32)
    key_doc = doc_index(key_pos, doc_ends)
    scores = (
        lax.dot_general(
            query_flat, block_rows, (((1,), (1,)), ((), ())), preferred_element_type=jnp.float32
        )
        * score_scale
    )
    allowed = (
        (key_pos[None, :] <= row_pos[:, None])
        & (key_pos[None, :] >= 0)
        & (key_doc[None, :] == row_doc[:, None])
    )
    new_peak = jnp.maximum(row_peak, jnp.max(jnp.where(allowed, scores, masked_score), axis=1))
    exponent = jnp.where(allowed, jnp.exp(scores - new_peak[:, None]), 0.0)
    row_total = jnp.sum(exponent, axis=1)
    weighted = jnp.dot(
        exponent.astype(jnp.bfloat16), block_rows[:, :lat_dim], preferred_element_type=jnp.float32
    )
    row_peak, row_total, weighted = (new_peak, row_total, weighted)
    context = (
        (weighted / row_total[:, None]).astype(jnp.bfloat16).reshape(tokens_dev, heads_dev, lat_dim)
    )
    head_out = jnp.einsum(
        "thl,hlv->thv", context, value_up, preferred_element_type=jnp.float32
    ).astype(jnp.bfloat16)
    head_out = head_out.reshape(tokens_dev, heads_dev * value_up.shape[2])
    mixed = lax.psum_scatter(
        jnp.dot(head_out, out_proj, preferred_element_type=jnp.float32).astype(jnp.bfloat16),
        "head",
        scatter_dimension=0,
        tiled=True,
    )
    return (kda_out, mixed[None])


def solution(mesh):
    placed = (
        P(("group", "req"), "ctx", "head"),
        P(("group", "req"), "ctx", "head"),
        P(("group", "req"), "ctx", "head"),
        P(("group", "req"), "ctx", "head"),
        P(("group", "req"), "head", "ctx"),
        P(("group", "req"), "ctx", "head"),
        P(("group", "req"), "ctx", None),
        P("head", None, None),
        P("head", None),
        P(("group", "req"), None),
    )
    return jax.shard_map(
        local,
        mesh=mesh,
        in_specs=placed,
        out_specs=(P(("group", "req"), "ctx", "head"), P(("group", "req"), ("ctx", "head"), None)),
        check_vma=False,
    )
```

profile of v0, /device:TPU:0, one launch (start us, length us, event | category | flops | bytes accessed | tf_op | source)
XLA Modules:
  0.0 443.5 jit_solution(2530594987979370844)
XLA Ops:
  8.8 23.7 %all_gather.3 = bf16[1,768,576]{2,1,0:T(8,128)(2,1)S(1)} all-gather(bf16[1,192,576]{2,1,0:T(8,128)(2,1)} %param.20), channel_id=1, replica_groups=mesh['group'=2,'ctx'=4,'head'=2,'req'=2] {'ctx'}, dimensions={1}, use_global_device_ids=true | all-gather | bytes 1105920 | tf_op jit(solution)/shard_map/all_gather | solution.py:166
  32.5 7.0 %reshape_squeeze.3 = bf16[3072,576]{1,0:T(8,128)(2,1)} reshape(bf16[1,192,9216]{2,1,0:T(8,128)(2,1)} %param.19) | data formatting | bytes 7077888 | tf_op jit(solution)/shard_map/reshape;squeeze | solution.py:161
  39.4 6.7 %select_reduce_fusion = (f32[3072]{0:T(1024)S(1)}, f32[3072,768]{0,1:T(8,128)S(1)}) fusion(s32[3072]{0:T(1024)S(1)} %eq.140, s32[3072]{0:T(1024)S(1)} %le.114, s32[768]{0:T(1024)S(1)} %convert_reduce_fusion, bf16[3072,576]{1,0:T(8,128)(2,1)} %reshape_squeeze.3, bf16[1,768,576]{2,1,0:T(8,128)(2,1)S(1)} %all_gather.3), kind=kOutput, calls=%fused_computation.7 | convolution fusion | flops 2732061696 | bytes 13900800 | tf_op jit(solution)/shard_map/dot_general | solution.py:171
  46.2 3.6 fusion.6
  49.8 4.3 divide_convert_fusion
  54.2 3.7 fusion.20
  57.9 3.0 convolution_convert_fusion
  75.2 80.0 %custom-call.8 = f32[16,1,64,64]{2,3,1,0:T(8,128)} custom-call(f32[16,1,64,64]{3,2,1,0:T(8,128)} %fusion.30), custom_call_target="InvertDiagBlocksLowerTriangular" | custom-call | tf_op jit(solution)/shard_map/triangular_solve/custom-call.1 | solution.py:49
  157.8 2.8 broadcast_multiply_fusion.2
  174.3 80.2 %custom-call.7 = f32[16,1,64,64]{2,3,1,0:T(8,128)} custom-call(f32[16,1,64,64]{3,2,1,0:T(8,128)} %fusion.35), custom_call_target="InvertDiagBlocksLowerTriangular" | custom-call | tf_op jit(solution)/shard_map/triangular_solve/custom-call.1 | solution.py:49
  256.9 2.9 fusion.66
  259.8 3.1 convolution_subtract_fusion.1
  264.7 80.2 %custom-call.6 = f32[16,1,64,64]{2,3,1,0:T(8,128)} custom-call(f32[16,1,64,64]{3,2,1,0:T(8,128)} %fusion.40), custom_call_target="InvertDiagBlocksLowerTriangular" | custom-call | tf_op jit(solution)/shard_map/triangular_solve/custom-call.1 | solution.py:49
  346.4 3.1 convolution_add_fusion.4
  353.9 3.0 convolution_add_fusion.3
  360.2 53.5 %while.11 = (s32[]{:T(128)}, f32[16,128,128]{2,1,0:T(8,128)S(1)}, f32[16,128,128]{2,1,0:T(8,128)}, f32[16,128,128]{2,1,0:T(8,128)}, s32[]{:T(128)}, /*index=5*/s32[]{:T(128)}) while((s32[]{:T(128)}, f32[16,128,128]{2,1,0:T(8,128)S(1)}, f32[16,128,128]{2,1,0:T(8,128)}, f32[16,128,128]{2,1,0:T(8,128)}, s32[]{:T(128)}, ...), condition=%wide.region_8.10_spmd.clone, body=%wide.region_7.9_spmd.clone.sunk | while | flops 403701760 | bytes 7340151 | solution.py:146
  360.2 3.5 fusion.158
  366.5 9.6 %collective-permute-done = bf16[16,128,128]{2,1,0:T(8,128)(2,1)} collective-permute-done((bf16[16,128,128]{2,1,0:T(8,128)(2,1)}, bf16[16,128,128]{2,1,0:T(8,128)(2,1)}, u32[]{:S(2)}, u32[]{:S(2)}) %collective-permute-start) | collective-permute-done | bytes 524320 | tf_op jit(solution)/shard_map/while/body/eval_jaxpr/ppermute | solution.py:17
  377.3 3.5 fusion.158
  380.8 5.2 %collective-permute-start = (bf16[16,128,128]{2,1,0:T(8,128)(2,1)}, bf16[16,128,128]{2,1,0:T(8,128)(2,1)}, u32[]{:S(2)}, u32[]{:S(2)}) collective-permute-start(bf16[16,128,128]{2,1,0:T(8,128)(2,1)} %fusion.158), channel_id=1, source_target_pairs={{0,4},{4,8},{8,12},{1,5},{5,9},{9,13},{2,6},{6,10},{10,14},{3,7},{... | collective-permute-start | bytes 1572872 | tf_op jit(solution)/shard_map/while/body/eval_jaxpr/ppermute | solution.py:17
  385.9 8.7 %collective-permute-done = bf16[16,128,128]{2,1,0:T(8,128)(2,1)} collective-permute-done((bf16[16,128,128]{2,1,0:T(8,128)(2,1)}, bf16[16,128,128]{2,1,0:T(8,128)(2,1)}, u32[]{:S(2)}, u32[]{:S(2)}) %collective-permute-start) | collective-permute-done | bytes 524320 | tf_op jit(solution)/shard_map/while/body/eval_jaxpr/ppermute | solution.py:17
  395.8 3.5 fusion.158
  399.3 5.2 %collective-permute-start = (bf16[16,128,128]{2,1,0:T(8,128)(2,1)}, bf16[16,128,128]{2,1,0:T(8,128)(2,1)}, u32[]{:S(2)}, u32[]{:S(2)}) collective-permute-start(bf16[16,128,128]{2,1,0:T(8,128)(2,1)} %fusion.158), channel_id=1, source_target_pairs={{0,4},{4,8},{8,12},{1,5},{5,9},{9,13},{2,6},{6,10},{10,14},{3,7},{... | collective-permute-start | bytes 1572872 | tf_op jit(solution)/shard_map/while/body/eval_jaxpr/ppermute | solution.py:17
  404.5 7.8 %collective-permute-done = bf16[16,128,128]{2,1,0:T(8,128)(2,1)} collective-permute-done((bf16[16,128,128]{2,1,0:T(8,128)(2,1)}, bf16[16,128,128]{2,1,0:T(8,128)(2,1)}, u32[]{:S(2)}, u32[]{:S(2)}) %collective-permute-start) | collective-permute-done | bytes 524320 | tf_op jit(solution)/shard_map/while/body/eval_jaxpr/ppermute | solution.py:17
  (152 shorter events, 71.8 us)
Async XLA Ops:
  7.2 47.0 %copy-start = (bf16[16,512,128]{2,1,0:T(8,128)(2,1)S(1)}, bf16[16,512,128]{2,1,0:T(8,128)(2,1)}, u32[]{:S(2)}) copy-start(bf16[16,512,128]{2,1,0:T(8,128)(2,1)} %param.21) | copy-start | bytes 6291460
  7.2 428.9 %reduce-scatter.2.cloned.1.call-start = ((), (), s32[]{:S(2)}) async-start(), calls=%async_computation.1 | async-start | bytes 1327104 | tf_op jit(solution)/shard_map/reduce_scatter | solution.py:195
  46.2 11.7 %slice-start = ((s8[9437184]{0:T(1024)(128)(4,1)}), s8[4194304]{0:T(1024)(128)(4,1)S(1)}, s32[]{:S(2)}) async-start(s8[9437184]{0:T(1024)(128)(4,1)} %bitcast.155), calls=%async_computation.2 | async-start | bytes 8388608
  49.8 8.1 %slice-start.1 = ((s8[9437184]{0:T(1024)(128)(4,1)}), s8[4194304]{0:T(1024)(128)(4,1)S(1)}, s32[]{:S(2)}) async-start(s8[9437184]{0:T(1024)(128)(4,1)} %bitcast.155), calls=%async_computation.3 | async-start | bytes 8388608
  49.8 8.1 %slice-start.2 = ((s8[9437184]{0:T(1024)(128)(4,1)}), s8[1048576]{0:T(1024)(128)(4,1)S(1)}, s32[]{:S(2)}) async-start(s8[9437184]{0:T(1024)(128)(4,1)} %bitcast.155), calls=%async_computation.4 | async-start | bytes 2097152
  57.9 3.6 copy-start.24
  61.7 7.9 %copy-start.28 = (f32[1,16,192]{2,1,0:T(8,128)S(1)}, f32[1,16,192]{2,1,0:T(8,128)}, u32[]{:S(2)}) copy-start(f32[1,16,192]{2,1,0:T(8,128)} %param.18) | copy-start | bytes 36868
  163.1 5.3 %copy-start.15 = (f32[16,64,256]{2,1,0:T(8,128)}, f32[16,64,256]{2,1,0:T(8,128)S(1)}, u32[]{:S(2)}) copy-start(f32[16,64,256]{2,1,0:T(8,128)S(1)} %fusion.52) | copy-start | bytes 3145732
  165.0 5.4 %copy-start.12 = (f32[16,128,128]{2,1,0:T(8,128)}, f32[16,128,128]{2,1,0:T(8,128)S(1)}, u32[]{:S(2)}) copy-start(f32[16,128,128]{2,1,0:T(8,128)S(1)} %fusion.68) | copy-start | bytes 3145732
  168.4 4.0 copy-start.8
  256.9 6.0 %copy-start.16 = (f32[16,64,256]{2,1,0:T(8,128)}, f32[16,64,256]{2,1,0:T(8,128)S(1)}, u32[]{:S(2)}) copy-start(f32[16,64,256]{2,1,0:T(8,128)S(1)} %fusion.48) | copy-start | bytes 3145732
  259.8 3.1 copy-start.5
  346.3 3.2 copy-start.22
  346.3 3.2 copy-start.23
  346.4 3.2 copy-start.27
  350.6 3.2 copy-start.18
  353.8 3.0 copy-start.10
  353.8 3.0 copy-start.20
  363.7 12.4 %collective-permute-start = (bf16[16,128,128]{2,1,0:T(8,128)(2,1)}, bf16[16,128,128]{2,1,0:T(8,128)(2,1)}, u32[]{:S(2)}, u32[]{:S(2)}) collective-permute-start(bf16[16,128,128]{2,1,0:T(8,128)(2,1)} %fusion.158), channel_id=1, source_target_pairs={{0,4},{4,8},{8,12},{1,5},{5,9},{9,13},{2,6},{6,10},{10,14},{3,7},{... | collective-permute-start | bytes 1572872 | tf_op jit(solution)/shard_map/while/body/eval_jaxpr/ppermute | solution.py:17
  380.8 13.9 %collective-permute-start = (bf16[16,128,128]{2,1,0:T(8,128)(2,1)}, bf16[16,128,128]{2,1,0:T(8,128)(2,1)}, u32[]{:S(2)}, u32[]{:S(2)}) collective-permute-start(bf16[16,128,128]{2,1,0:T(8,128)(2,1)} %fusion.158), channel_id=1, source_target_pairs={{0,4},{4,8},{8,12},{1,5},{5,9},{9,13},{2,6},{6,10},{10,14},{3,7},{... | collective-permute-start | bytes 1572872 | tf_op jit(solution)/shard_map/while/body/eval_jaxpr/ppermute | solution.py:17
  399.3 13.0 %collective-permute-start = (bf16[16,128,128]{2,1,0:T(8,128)(2,1)}, bf16[16,128,128]{2,1,0:T(8,128)(2,1)}, u32[]{:S(2)}, u32[]{:S(2)}) collective-permute-start(bf16[16,128,128]{2,1,0:T(8,128)(2,1)} %fusion.158), channel_id=1, source_target_pairs={{0,4},{4,8},{8,12},{1,5},{5,9},{9,13},{2,6},{6,10},{10,14},{3,7},{... | collective-permute-start | bytes 1572872 | tf_op jit(solution)/shard_map/while/body/eval_jaxpr/ppermute | solution.py:17
  413.7 2.4 copy-start.9
  413.7 2.4 copy-start.13
  432.5 3.6 copy-start.1
  (12 other events, 14.9 us)
Sparse Core Ops, SparseCore 0:
  61.1 18.3 reduce-scatter.1
where the time goes:
time: 449 us; the launch traced here: 443 us
  other arithmetic  261 us (58%)
  matrix products  84.7 us (19%)
  waiting for transfers between devices  26.2 us (6%)
  blocking collectives  23.7 us (5%)
  between operations  17.1 us (4%)
  local copies, waits for them, and re-layouts  16.8 us (4%)
  starting transfers between devices  13.2 us (3%)
    another operation x5, other arithmetic, span_terms(): lax.linalg.triangular_solve(system, right_side, left_side=True, lower=Tru...  240 us
    ppermute x3, waiting for transfers between devices, from_behind(): return lax.ppermute(value, axis, pairs)  26.2 us
    all_gather x1, blocking collectives, local(): block_rows = lax.all_gather(latents, 'ctx', axis=1, tiled=True)[0]  23.7 us
    dot_general x8, matrix products, apply_map(): jnp.einsum('hcd,hdv->hcv', transition, inbound_state, precision=top_value)  19.1 us
    ppermute x3, starting transfers between devices, from_behind(): return lax.ppermute(value, axis, pairs)  13.1 us
  transfers between devices with their start and end apart: 4, of which 3 were waited for; matrix products, arithmetic and copies ran while one was open for 75% of the time, Pallas kernels for 0%

commit v1 on v0

--- a/solution.py
+++ b/solution.py
@@ -163,7 +163,9 @@
     row_doc = jnp.repeat(doc_ids, heads_dev)
     row_total_count = tokens_dev * heads_dev
     row_peak = jnp.full((row_total_count,), masked_score, jnp.float32)
-    block_rows = lax.all_gather(latents, "ctx", axis=1, tiled=True)[0]
+    block_rows = jnp.concatenate(
+        lax.all_to_all(jnp.stack([latents] * lax.axis_size("ctx")), "ctx", 0, 0), axis=1
+    )[0]
     row_count = block_rows.shape[0]
     key_pos = jnp.arange(row_count, dtype=jnp.int32)
     key_doc = doc_index(key_pos, doc_ends)

time: 449 us -> 463 us (1.031)
  blocking collectives: 23.7 us -> 0 us
  matrix products: 84.7 us -> 99 us
  waiting for transfers between devices: 26.2 us -> 35.5 us
  starting transfers between devices: 13.2 us -> 21.4 us
  local copies, waits for them, and re-layouts: 16.8 us -> 23.1 us
    all_gather x1 -> x0, blocking collectives: 23.7 us -> none  [local(): block_rows = lax.all_gather(latents, 'ctx', axis=1, tiled=True)[0]]
    reduce_scatter x1, waiting for transfers between devices: 0.01 us -> 7.89 us  [local(): lax.psum_scatter(jnp.dot(head_out, out_proj, preferred_element_type=jnp.f...]
    all_to_all x0 -> x1, starting transfers between devices: none -> 6.32 us  [local(): lax.all_to_all(jnp.stack([latents] * lax.axis_size('ctx')), 'ctx', 0, 0)]
  transfers between devices with their start and end apart: 4 -> 5, of which waited for: 3 -> 4; matrix products, arithmetic and copies ran while one was open for 75% -> 77% of each run, Pallas kernels for 0% -> 0%
where the time goes in v1:
time: 463 us; the launch traced here: 458 us
  other arithmetic  261 us (56%)
  matrix products  99 us (21%)
  waiting for transfers between devices  35.5 us (8%)
  local copies, waits for them, and re-layouts  23.1 us (5%)
  starting transfers between devices  21.4 us (5%)
  between operations  17.5 us (4%)
    another operation x5, other arithmetic, span_terms(): lax.linalg.triangular_solve(system, right_side, left_side=True, lower=Tru...  241 us
    ppermute x3, waiting for transfers between devices, from_behind(): return lax.ppermute(value, axis, pairs)  27.6 us
    dot_general x8, matrix products, apply_map(): jnp.einsum('hcd,hdv->hcv', transition, inbound_state, precision=top_value)  21.5 us
    ppermute x3, starting transfers between devices, from_behind(): return lax.ppermute(value, axis, pairs)  15.1 us
  transfers between devices with their start and end apart: 5, of which 4 were waited for; matrix products, arithmetic and copies ran while one was open for 77% of the time, Pallas kernels for 0%

profile of v1, /device:TPU:0, one launch (start us, length us, event | category | flops | bytes accessed | tf_op | source)
XLA Modules:
  0.0 457.6 jit_solution(15465716919965113255)
XLA Ops:
  9.3 6.3 %all-to-all-start = ((bf16[4,1,192,576]{3,2,1,0:T(8,128)(2,1)}), bf16[4,1,192,576]{3,2,1,0:T(8,128)(2,1)}, u32[]{:S(2)}, u32[]{:S(2)}) async-start(bf16[4,1,192,576]{3,2,1,0:T(8,128)(2,1)} %stack.2), calls=%async_computation | async-start | bytes 1966080 | tf_op jit(solution)/shard_map/all_to_all | solution.py:167
  32.7 80.2 %custom-call.8 = f32[16,1,64,64]{2,3,1,0:T(8,128)} custom-call(f32[16,1,64,64]{3,2,1,0:T(8,128)} %fusion.30), custom_call_target="InvertDiagBlocksLowerTriangular" | custom-call | tf_op jit(solution)/shard_map/triangular_solve/custom-call.1 | solution.py:49
  132.6 80.2 %custom-call.7 = f32[16,1,64,64]{2,3,1,0:T(8,128)} custom-call(f32[16,1,64,64]{3,2,1,0:T(8,128)} %fusion.35), custom_call_target="InvertDiagBlocksLowerTriangular" | custom-call | tf_op jit(solution)/shard_map/triangular_solve/custom-call.1 | solution.py:49
  218.4 3.0 convolution_subtract_fusion.1
  223.4 80.5 %custom-call.6 = f32[16,1,64,64]{2,3,1,0:T(8,128)} custom-call(f32[16,1,64,64]{3,2,1,0:T(8,128)} %fusion.40), custom_call_target="InvertDiagBlocksLowerTriangular" | custom-call | tf_op jit(solution)/shard_map/triangular_solve/custom-call.1 | solution.py:49
  305.4 3.1 convolution_add_fusion.4
  319.5 56.8 %while.11 = (s32[]{:T(128)}, f32[16,128,128]{2,1,0:T(8,128)S(1)}, f32[16,128,128]{2,1,0:T(8,128)}, f32[16,128,128]{2,1,0:T(8,128)}, s32[]{:T(128)}, /*index=5*/s32[]{:T(128)}) while((s32[]{:T(128)}, f32[16,128,128]{2,1,0:T(8,128)S(1)}, f32[16,128,128]{2,1,0:T(8,128)}, f32[16,128,128]{2,1,0:T(8,128)}, s32[]{:T(128)}, ...), condition=%wide.region_8.10_spmd.clone, body=%wide.region_7.9_spmd.clone.sunk | while | flops 403701760 | bytes 7340151 | solution.py:146
  319.5 3.5 fusion.157
  323.0 4.7 %collective-permute-start = (bf16[16,128,128]{2,1,0:T(8,128)(2,1)}, bf16[16,128,128]{2,1,0:T(8,128)(2,1)}, u32[]{:S(2)}, u32[]{:S(2)}) collective-permute-start(bf16[16,128,128]{2,1,0:T(8,128)(2,1)} %fusion.157), channel_id=1, source_target_pairs={{0,4},{4,8},{8,12},{1,5},{5,9},{9,13},{2,6},{6,10},{10,14},{3,7},{... | collective-permute-start | bytes 1572872 | tf_op jit(solution)/shard_map/while/body/eval_jaxpr/ppermute | solution.py:17
  327.7 10.1 %collective-permute-done = bf16[16,128,128]{2,1,0:T(8,128)(2,1)} collective-permute-done((bf16[16,128,128]{2,1,0:T(8,128)(2,1)}, bf16[16,128,128]{2,1,0:T(8,128)(2,1)}, u32[]{:S(2)}, u32[]{:S(2)}) %collective-permute-start) | collective-permute-done | bytes 524320 | tf_op jit(solution)/shard_map/while/body/eval_jaxpr/ppermute | solution.py:17
  339.0 3.5 fusion.157
  342.5 5.2 %collective-permute-start = (bf16[16,128,128]{2,1,0:T(8,128)(2,1)}, bf16[16,128,128]{2,1,0:T(8,128)(2,1)}, u32[]{:S(2)}, u32[]{:S(2)}) collective-permute-start(bf16[16,128,128]{2,1,0:T(8,128)(2,1)} %fusion.157), channel_id=1, source_target_pairs={{0,4},{4,8},{8,12},{1,5},{5,9},{9,13},{2,6},{6,10},{10,14},{3,7},{... | collective-permute-start | bytes 1572872 | tf_op jit(solution)/shard_map/while/body/eval_jaxpr/ppermute | solution.py:17
  347.7 9.2 %collective-permute-done = bf16[16,128,128]{2,1,0:T(8,128)(2,1)} collective-permute-done((bf16[16,128,128]{2,1,0:T(8,128)(2,1)}, bf16[16,128,128]{2,1,0:T(8,128)(2,1)}, u32[]{:S(2)}, u32[]{:S(2)}) %collective-permute-start) | collective-permute-done | bytes 524320 | tf_op jit(solution)/shard_map/while/body/eval_jaxpr/ppermute | solution.py:17
  358.0 3.5 fusion.157
  361.5 5.2 %collective-permute-start = (bf16[16,128,128]{2,1,0:T(8,128)(2,1)}, bf16[16,128,128]{2,1,0:T(8,128)(2,1)}, u32[]{:S(2)}, u32[]{:S(2)}) collective-permute-start(bf16[16,128,128]{2,1,0:T(8,128)(2,1)} %fusion.157), channel_id=1, source_target_pairs={{0,4},{4,8},{8,12},{1,5},{5,9},{9,13},{2,6},{6,10},{10,14},{3,7},{... | collective-permute-start | bytes 1572872 | tf_op jit(solution)/shard_map/while/body/eval_jaxpr/ppermute | solution.py:17
  366.7 8.3 %collective-permute-done = bf16[16,128,128]{2,1,0:T(8,128)(2,1)} collective-permute-done((bf16[16,128,128]{2,1,0:T(8,128)(2,1)}, bf16[16,128,128]{2,1,0:T(8,128)(2,1)}, u32[]{:S(2)}, u32[]{:S(2)}) %collective-permute-start) | collective-permute-done | bytes 524320 | tf_op jit(solution)/shard_map/while/body/eval_jaxpr/ppermute | solution.py:17
  387.2 7.1 %reshape_squeeze.3 = bf16[3072,576]{1,0:T(8,128)(2,1)} reshape(bf16[1,192,9216]{2,1,0:T(8,128)(2,1)} %param.19) | data formatting | bytes 7077888 | tf_op jit(solution)/shard_map/reshape;squeeze | solution.py:161
  394.4 3.5 convolution_subtract_fusion.4
  403.5 3.0 convolution_select_fusion.1
  406.5 7.0 %select_reduce_fusion = (f32[3072]{0:T(1024)S(1)}, f32[3072,768]{0,1:T(8,128)S(1)}) fusion(s32[3072]{0:T(1024)S(1)} %eq.140, s32[3072]{0:T(1024)S(1)} %le.114, s32[768]{0:T(1024)S(1)} %convert_reduce_fusion, bf16[3072,576]{1,0:T(8,128)(2,1)} %reshape_squeeze.3, bf16[768,576]{1,0:T(8,128)(2,1)} %bitcast.36), kind=kOutput, calls=%fused_computation.7 | convolution fusion | flops 2732061696 | bytes 13900800 | tf_op jit(solution)/shard_map/dot_general | solution.py:173
  413.5 3.7 fusion.6
  417.2 5.6 %divide_convert_fusion = bf16[3072,512]{1,0:T(8,128)(2,1)S(1)} fusion(f32[3072]{0:T(1024)S(1)} %fusion.6, f32[3072,768]{0,1:T(8,128)S(1)} %get-tuple-element.87, f32[3072]{0:T(1024)S(1)} %broadcast_maximum_fusion, s32[3072]{0:T(1024)S(1)} %eq.140, s32[3072]{0:T(1024)S(1)} %le.114, s32[768]{0:T(1024)S(1)} %convert_reduce_fusion, bf16[768,576]{1,0:T(8,128)(2,1)} %bitcast.36), kind=kOutput, calls=%fused_computation.10 | convolution fusion | flops 2435579904 | bytes 13421568 | tf_op jit(solution)/shard_map/dot_general | solution.py:186
  422.9 3.7 fusion.20
  442.3 7.9 %reduce-scatter.2.cloned.1.call-done = bf16[96,2304]{1,0:T(8,128)(2,1)} async-done(((bf16[192,2304]{1,0:T(8,128)(2,1)}), bf16[96,2304]{1,0:T(8,128)(2,1)}) %reduce-scatter.2.cloned.1.call-update) | async-done | bytes 442384 | tf_op jit(solution)/shard_map/reduce_scatter | solution.py:197
  (182 shorter events, 91.8 us)
Async XLA Ops:
  7.2 415.7 %copy-start = (bf16[16,512,128]{2,1,0:T(8,128)(2,1)S(1)}, bf16[16,512,128]{2,1,0:T(8,128)(2,1)}, u32[]{:S(2)}) copy-start(bf16[16,512,128]{2,1,0:T(8,128)(2,1)} %param.21) | copy-start | bytes 6291460
  9.3 397.2 %all-to-all-start = ((bf16[4,1,192,576]{3,2,1,0:T(8,128)(2,1)}), bf16[4,1,192,576]{3,2,1,0:T(8,128)(2,1)}, u32[]{:S(2)}, u32[]{:S(2)}) async-start(bf16[4,1,192,576]{3,2,1,0:T(8,128)(2,1)} %stack.2), calls=%async_computation | async-start | bytes 1966080 | tf_op jit(solution)/shard_map/all_to_all | solution.py:167
  15.6 434.6 %reduce-scatter.2.cloned.1.call-start = ((), (), s32[]{:S(2)}) async-start(), calls=%async_computation.2 | async-start | bytes 1327104 | tf_op jit(solution)/shard_map/reduce_scatter | solution.py:197
  16.9 5.0 %copy-start.42 = (s32[1,8]{1,0:T(1,128)S(1)}, s32[1,8]{1,0:T(1,128)}, u32[]{:S(2)}) copy-start(s32[1,8]{1,0:T(1,128)} %param.23) | copy-start | bytes 100
  16.9 9.8 %copy-start.41 = (f32[1,16,192]{2,1,0:T(8,128)S(1)}, f32[1,16,192]{2,1,0:T(8,128)}, u32[]{:S(2)}) copy-start(f32[1,16,192]{2,1,0:T(8,128)} %param.18) | copy-start | bytes 36868
  121.5 5.3 %copy-start.29 = (f32[16,64,256]{2,1,0:T(8,128)}, f32[16,64,256]{2,1,0:T(8,128)S(1)}, u32[]{:S(2)}) copy-start(f32[16,64,256]{2,1,0:T(8,128)S(1)} %fusion.52) | copy-start | bytes 3145732
  123.4 5.4 %copy-start.24 = (f32[16,128,128]{2,1,0:T(8,128)}, f32[16,128,128]{2,1,0:T(8,128)S(1)}, u32[]{:S(2)}) copy-start(f32[16,128,128]{2,1,0:T(8,128)S(1)} %fusion.68) | copy-start | bytes 3145732
  126.8 4.0 copy-start.16
  215.5 6.0 %copy-start.28 = (f32[16,64,256]{2,1,0:T(8,128)}, f32[16,64,256]{2,1,0:T(8,128)S(1)}, u32[]{:S(2)}) copy-start(f32[16,64,256]{2,1,0:T(8,128)S(1)} %fusion.48) | copy-start | bytes 3145732
  305.4 3.2 copy-start.35
  309.6 3.6 copy-start.30
  323.0 14.8 %collective-permute-start = (bf16[16,128,128]{2,1,0:T(8,128)(2,1)}, bf16[16,128,128]{2,1,0:T(8,128)(2,1)}, u32[]{:S(2)}, u32[]{:S(2)}) collective-permute-start(bf16[16,128,128]{2,1,0:T(8,128)(2,1)} %fusion.157), channel_id=1, source_target_pairs={{0,4},{4,8},{8,12},{1,5},{5,9},{9,13},{2,6},{6,10},{10,14},{3,7},{... | collective-permute-start | bytes 1572872 | tf_op jit(solution)/shard_map/while/body/eval_jaxpr/ppermute | solution.py:17
  342.5 14.4 %collective-permute-start = (bf16[16,128,128]{2,1,0:T(8,128)(2,1)}, bf16[16,128,128]{2,1,0:T(8,128)(2,1)}, u32[]{:S(2)}, u32[]{:S(2)}) collective-permute-start(bf16[16,128,128]{2,1,0:T(8,128)(2,1)} %fusion.157), channel_id=1, source_target_pairs={{0,4},{4,8},{8,12},{1,5},{5,9},{9,13},{2,6},{6,10},{10,14},{3,7},{... | collective-permute-start | bytes 1572872 | tf_op jit(solution)/shard_map/while/body/eval_jaxpr/ppermute | solution.py:17
  361.5 13.5 %collective-permute-start = (bf16[16,128,128]{2,1,0:T(8,128)(2,1)}, bf16[16,128,128]{2,1,0:T(8,128)(2,1)}, u32[]{:S(2)}, u32[]{:S(2)}) collective-permute-start(bf16[16,128,128]{2,1,0:T(8,128)(2,1)} %fusion.157), channel_id=1, source_target_pairs={{0,4},{4,8},{8,12},{1,5},{5,9},{9,13},{2,6},{6,10},{10,14},{3,7},{... | collective-permute-start | bytes 1572872 | tf_op jit(solution)/shard_map/while/body/eval_jaxpr/ppermute | solution.py:17
  382.7 4.1 copy-start.22
  394.3 3.6 copy-start.19
  394.3 3.6 copy-start.20
  397.9 3.6 copy-start.31
  413.5 13.0 %slice-start = ((s8[9437184]{0:T(1024)(128)(4,1)}), s8[4194304]{0:T(1024)(128)(4,1)S(1)}, s32[]{:S(2)}) async-start(s8[9437184]{0:T(1024)(128)(4,1)} %bitcast.153), calls=%async_computation.3 | async-start | bytes 8388608
  417.2 9.4 %slice-start.1 = ((s8[9437184]{0:T(1024)(128)(4,1)}), s8[4194304]{0:T(1024)(128)(4,1)S(1)}, s32[]{:S(2)}) async-start(s8[9437184]{0:T(1024)(128)(4,1)} %bitcast.153), calls=%async_computation.4 | async-start | bytes 8388608
  417.2 9.4 %slice-start.2 = ((s8[9437184]{0:T(1024)(128)(4,1)}), s8[1048576]{0:T(1024)(128)(4,1)S(1)}, s32[]{:S(2)}) async-start(s8[9437184]{0:T(1024)(128)(4,1)} %bitcast.153), calls=%async_computation.5 | async-start | bytes 2097152
  431.6 3.4 copy-start.12
  431.6 3.4 copy-start.23
  431.6 3.4 copy-start.34
  (27 other events, 52.6 us)
Sparse Core Ops, SparseCore 0:
  429.8 20.4 reduce-scatter.1
